TPU v7x, 32 devices: a whole 2x2x4 slice. The times are simulated.
32 devices in a mesh: grp: 4 (over y, x), space: 8 (over z, core).
Axes of the slice: x: 2, y: 2, z: 4, core: 2. Of those that a mesh axis runs over, the one named last changes fastest.
Arguments:
- features: bfloat16 [4, 128, 128, 128], P('grp', 'space'), may hold values from -6 to 6
- weights: bfloat16 [27, 128, 128], replicated, may hold values from -0.109375 to 0.109375
- cotangent: bfloat16 [4, 128, 128, 128], P('grp', 'space'), may hold values from -6 to 6
- kernel_map: int32 [4, 128, 27], P('grp', 'space'), may hold values from -1 to 127, as said below
- counts: int32 [4, 8], P('grp', 'space'), may hold values from 4 to 16
Outputs:
- output: bfloat16 [4, 128, 128, 128], P('grp', 'space')
- input_grad: bfloat16 [4, 128, 128, 128], P('grp', 'space')
- weight_grad: float32 [3456, 128], P('space')
Inputs may be any that keep to these rules, and one draw needn't show every extreme that they name: `kernel_map`: the centre offset k = 27 div 2 maps every block to itself. Otherwise an entry for an output block b on slab d = b div 16 is -1 or lies in [d * 16 - 4, (d + 1) * 16 + 4) within the sample. The live blocks of a device are its first counts slots.
All inputs are finite; a program needn't handle non-finite values.
Results may differ from a plain program's by a relative error of at most 0.005.
Values may be sent and summed in bfloat16 or wider, within the bound.
A program may use at most 64 MiB of HBM per device.

v0:
```python
import jax
import jax.numpy as jnp
from jax import lax
from jax.sharding import PartitionSpec as P

K = 27
H = 4


def extended_2(block, sides, width):
    for axis, dim in sides:
        count = lax.axis_size(axis)
        forward = [(i, i + 1) for i in range(count - 1)]
        backward = [(target, source) for source, target in forward]
        low = lax.ppermute(
            lax.slice_in_dim(block, block.shape[dim] - width, None, axis=dim), axis, forward
        )
        high = lax.ppermute(lax.slice_in_dim(block, 0, width, axis=dim), axis, backward)
        block = jnp.concatenate([low, block, high], axis=dim)
    return block


def passed_along(block, axis, distance):
    devices = range(lax.axis_size(axis))
    route = [(i - distance, i) for i in devices if i - distance in devices]
    return lax.ppermute(block, axis, route)


def per_device(features, weights, cotangent, kernel_map, counts):
    voxels = features[0]
    slots = voxels.shape[0]
    device = lax.axis_index("space")
    live_mask = (jnp.arange(slots) < counts[0, 0]).astype(jnp.bfloat16)[:, None, None]
    live_float = live_mask.astype(jnp.float32)
    masked = voxels * live_mask
    grad_out = cotangent[0] * live_mask
    extended = extended_2(masked, (("space", 0),), H)
    block_map = kernel_map[0]
    first_block = device * slots - H
    present = (block_map >= 0).astype(jnp.bfloat16)
    local_index = jnp.where(block_map >= 0, block_map - first_block, 0)
    channels_in = voxels.shape[2]
    channels_out = weights.shape[2]

    def step(offset, carry):
        total, grad_in, wgrad = carry
        column = lax.dynamic_index_in_dim(local_index, offset, 1, keepdims=False)
        present_k = lax.dynamic_index_in_dim(present, offset, 1, keepdims=False)[:, None, None]
        gathered = jnp.take(extended, column, axis=0) * present_k
        kernel = lax.dynamic_index_in_dim(weights, offset, 0, keepdims=False)
        total = total + jnp.einsum(
            "brc,co->bro", gathered, kernel, preferred_element_type=jnp.float32
        )
        term = jnp.einsum("bro,co->brc", grad_out, kernel, preferred_element_type=jnp.float32)
        grad_in = grad_in.at[column].add(term * present_k.astype(jnp.float32))
        piece = jnp.einsum("brc,bro->co", gathered, grad_out, preferred_element_type=jnp.float32)
        wgrad = lax.dynamic_update_index_in_dim(wgrad, piece, offset, 0)
        return (total, grad_in, wgrad)

    start = (
        jnp.zeros((slots, voxels.shape[1], channels_out), jnp.float32),
        jnp.zeros((slots + 2 * H, voxels.shape[1], channels_in), jnp.float32),
        jnp.zeros((K, channels_in, channels_out), jnp.float32),
    )
    total, grad_in, wgrad = lax.fori_loop(0, K, step, start)
    output = (total * live_float).astype(jnp.bfloat16)
    lower_rim = grad_in[:H]
    upper_rim = grad_in[slots + H :]
    own_grad = grad_in[H : slots + H]
    from_above = passed_along(lower_rim.astype(jnp.bfloat16), "space", -1).astype(lower_rim.dtype)
    from_below = passed_along(upper_rim.astype(jnp.bfloat16), "space", 1).astype(upper_rim.dtype)
    own_grad = own_grad.at[:H].add(from_below)
    own_grad = own_grad.at[slots - H :].add(from_above)
    input_grad = (own_grad * live_float).astype(jnp.bfloat16)
    weight_rows = wgrad.reshape(K * channels_in, channels_out)
    summed = lax.psum(weight_rows, ("grp", "space"))
    row_count = weight_rows.shape[0] // lax.axis_size("space")
    own_rows = lax.dynamic_slice_in_dim(summed, device * row_count, row_count, 0)
    return (output[None], input_grad[None], own_rows)


def solution(mesh):
    in_specs = (
        P("grp", "space", None, None),
        P(),
        P("grp", "space", None, None),
        P("grp", "space", None),
        P("grp", "space"),
    )
    out_specs = (P("grp", "space", None, None), P("grp", "space", None, None), P("space", None))
    return jax.shard_map(
        per_device, mesh=mesh, in_specs=in_specs, out_specs=out_specs, check_vma=False
    )
```

profile of v0, /device:TPU:0, one launch (start us, length us, event | category | flops | bytes accessed | tf_op | source)
XLA Modules:
  0.0 446.6 jit_solution(6604111132095993957)
XLA Ops:
  13.1 4.0 collective-permute-done.1
  19.4 278.4 %while.20 = (s32[]{:T(128)}, f32[16,128,128]{2,1,0:T(8,128)}, f32[24,128,128]{2,1,0:T(8,128)}, f32[27,128,128]{2,1,0:T(8,128)}, s32[16,27]{0,1:T(8,128)S(1)}, /*...) while((s32[]{:T(128)}, f32[16,128,128]{2,1,0:T(8,128)}, ...), condition=%wide.region_2.3_spmd.clone, body=%wide.region_0.2_spmd.clone.sunk | while | flops 203424880 | bytes 11670275 | solution.py:65
  24.7 3.5 scatter_fusion
  35.2 3.4 scatter_fusion
  45.6 3.3 scatter_fusion
  55.9 3.4 scatter_fusion
  97.1 3.4 scatter_fusion
  107.5 3.3 scatter_fusion
  117.8 3.3 scatter_fusion
  138.3 3.4 scatter_fusion
  158.9 3.4 scatter_fusion
  179.6 3.4 scatter_fusion
  189.9 3.4 scatter_fusion
  200.3 3.4 scatter_fusion
  210.6 3.4 scatter_fusion
  220.9 3.4 scatter_fusion
  231.2 3.4 scatter_fusion
  241.6 3.3 scatter_fusion
  251.9 3.4 scatter_fusion
  262.3 3.3 scatter_fusion
  272.6 3.4 scatter_fusion
  293.2 3.4 scatter_fusion
  299.4 6.2 %collective-permute-start.2 = (bf16[4,128,128]{2,1,0:T(8,128)(2,1)S(1)}, bf16[4,128,128]{2,1,0:T(8,128)(2,1)S(1)}, u32[]{:S(2)}, u32[]{:S(2)}) collective-permute-start(bf16[4,128,128]{2,1,0:T(8,128)(2,1)S(1)} %get-tuple-element.239), channel_id=1, source_target_pairs={{0,1},{1,2},{2,3},{3,4},{4,5},{5,6},{6,7},{8,9},{9,10},{10,11},{11... | collective-permute-start | bytes 393224 | tf_op jit(solution)/shard_map/ppermute | solution.py:26
  311.6 126.6 %all-reduce.2.cloned.1.call-done = f32[3456,128]{1,0:T(8,128)} async-done(((f32[3456,128]{1,0:T(8,128)}), f32[3456,128]{1,0:T(8,128)}) %all-reduce.2.cloned.1.call-update) | async-done | bytes 1769488 | tf_op jit(solution)/shard_map/psum | solution.py:76
  (253 shorter events, 226.5 us)
Async XLA Ops:
  7.2 5.8 %copy-start.1 = (s32[1,16,27]{2,1,0:T(8,128)S(1)}, s32[1,16,27]{2,1,0:T(8,128)}, u32[]{:S(2)}) copy-start(s32[1,16,27]{2,1,0:T(8,128)} %param.14) | copy-start | bytes 5188
  7.2 431.0 %all-reduce.2.cloned.1.call-start = ((), (), s32[]{:S(2)}) async-start(), calls=%async_computation | async-start | bytes 3538944 | tf_op jit(solution)/shard_map/psum | solution.py:76
  9.2 3.8 collective-permute-start
  11.7 5.4 %collective-permute-start.1 = (bf16[4,128,128]{2,1,0:T(8,128)(2,1)S(1)}, bf16[4,128,128]{2,1,0:T(8,128)(2,1)S(1)}, u32[]{:S(2)}, u32[]{:S(2)}) collective-permute-start(bf16[4,128,128]{2,1,0:T(8,128)(2,1)S(1)} %get-tuple-element.241), channel_id=1, source_target_pairs={{1,0},{2,1},{3,2},{4,3},{5,4},{6,5},{7,6},{9,8},{10,9},{11,10},{12... | collective-permute-start | bytes 393224 | tf_op jit(solution)/shard_map/ppermute | solution.py:18
  297.7 7.9 %copy-start = (f32[24,128,128]{2,1,0:T(8,128)S(1)}, f32[24,128,128]{2,1,0:T(8,128)}, u32[]{:S(2)}) copy-start(f32[24,128,128]{2,1,0:T(8,128)} %get-tuple-element.184) | copy-start | bytes 4718596
  299.4 7.6 %collective-permute-start.2 = (bf16[4,128,128]{2,1,0:T(8,128)(2,1)S(1)}, bf16[4,128,128]{2,1,0:T(8,128)(2,1)S(1)}, u32[]{:S(2)}, u32[]{:S(2)}) collective-permute-start(bf16[4,128,128]{2,1,0:T(8,128)(2,1)S(1)} %get-tuple-element.239), channel_id=1, source_target_pairs={{0,1},{1,2},{2,3},{3,4},{4,5},{5,6},{6,7},{8,9},{9,10},{10,11},{11... | collective-permute-start | bytes 393224 | tf_op jit(solution)/shard_map/ppermute | solution.py:26
  305.8 3.2 collective-permute-start.3
Sparse Core Ops, SparseCore 0:
  305.8 132.3 all-reduce.1
where the time goes:
time: 453 us; the launch traced here: 447 us
  waiting for transfers between devices  132 us (29%)
  matrix products  129 us (28%)
  other arithmetic  98.1 us (22%)
  local copies, waits for them, and re-layouts  60.2 us (13%)
  between operations  14.8 us (3%)
  starting transfers between devices  11.2 us (2%)
    psum x1, waiting for transfers between devices, per_device(): summed = lax.psum(weight_rows, ('grp', 'space'))  127 us
    scatter-add x27, other arithmetic, step(): grad_in = grad_in.at[column].add(term * present_k.astype(jnp.float32))  90.8 us
    dot_general x27, matrix products, step(): jnp.einsum('brc,co->bro', gathered, kernel, preferred_element_type=jnp.fl...  70 us
    gather x27, local copies, waits for them, and re-layouts, step(): gathered = jnp.take(extended, column, axis=0) * present_k  48.1 us
    dot_general x27, matrix products, step(): jnp.einsum('brc,bro->co', gathered, grad_out, preferred_element_type=jnp....  30.5 us
    dot_general x27, matrix products, step(): jnp.einsum('bro,co->brc', grad_out, kernel, preferred_element_type=jnp.fl...  28.4 us
  transfers between devices with their start and end apart: 5, of which 3 were waited for; matrix products, arithmetic and copies ran while one was open for 1% of the time, Pallas kernels for 0%

commit v1 on v0

--- a/solution.py
+++ b/solution.py
@@ -73,7 +73,7 @@
     own_grad = own_grad.at[slots - H :].add(from_above)
     input_grad = (own_grad * live_float).astype(jnp.bfloat16)
     weight_rows = wgrad.reshape(K * channels_in, channels_out)
-    summed = lax.psum(weight_rows, ("grp", "space"))
+    summed = lax.psum(lax.psum(weight_rows, "space"), "grp")
     row_count = weight_rows.shape[0] // lax.axis_size("space")
     own_rows = lax.dynamic_slice_in_dim(summed, device * row_count, row_count, 0)
     return (output[None], input_grad[None], own_rows)

time: 453 us -> 446 us (0.985)
  starting transfers between devices: 11.2 us -> 6.36 us
    ppermute x2, starting transfers between devices: 7.46 us -> 2.59 us  [passed_along(): return lax.ppermute(block, axis, route)]
    psum x1 -> x2, waiting for transfers between devices: 127 us -> 125 us  [per_device(): summed = lax.psum(lax.psum(weight_rows, 'space'), 'grp')]
  transfers between devices with their start and end apart: 5 -> 6, of which waited for: 3 -> 4; matrix products, arithmetic and copies ran while one was open for 1% -> 1% of each run, Pallas kernels for 0% -> 0%
where the time goes in v1:
time: 446 us; the launch traced here: 440 us
  waiting for transfers between devices  132 us (30%)
  matrix products  129 us (29%)
  other arithmetic  96.6 us (22%)
  local copies, waits for them, and re-layouts  60.2 us (13%)
  between operations  14.9 us (3%)
  starting transfers between devices  6.36 us (1%)
    psum x2, waiting for transfers between devices, per_device(): summed = lax.psum(lax.psum(weight_rows, 'space'), 'grp')  125 us
    scatter-add x27, other arithmetic, step(): grad_in = grad_in.at[column].add(term * present_k.astype(jnp.float32))  90.8 us
    dot_general x27, matrix products, step(): jnp.einsum('brc,co->bro', gathered, kernel, preferred_element_type=jnp.fl...  70 us
    gather x27, local copies, waits for them, and re-layouts, step(): gathered = jnp.take(extended, column, axis=0) * present_k  48.1 us
    dot_general x27, matrix products, step(): jnp.einsum('brc,bro->co', gathered, grad_out, preferred_element_type=jnp....  30.5 us
    dot_general x27, matrix products, step(): jnp.einsum('bro,co->brc', grad_out, kernel, preferred_element_type=jnp.fl...  28.4 us
    mul x27, local copies, waits for them, and re-layouts, step(): grad_in = grad_in.at[column].add(term * present_k.astype(jnp.float32))  8.94 us
  transfers between devices with their start and end apart: 6, of which 4 were waited for; matrix products, arithmetic and copies ran while one was open for 1% of the time, Pallas kernels for 0%

profile of v1, /device:TPU:0, one launch (start us, length us, event | category | flops | bytes accessed | tf_op | source)
XLA Modules:
  0.0 439.7 jit_solution(11190660362098154049)
XLA Ops:
  13.1 4.0 collective-permute-done.1
  19.4 278.4 %while.20 = (s32[]{:T(128)}, f32[16,128,128]{2,1,0:T(8,128)}, f32[24,128,128]{2,1,0:T(8,128)}, f32[27,128,128]{2,1,0:T(8,128)}, s32[16,27]{0,1:T(8,128)S(1)}, /*...) while((s32[]{:T(128)}, f32[16,128,128]{2,1,0:T(8,128)}, ...), condition=%wide.region_2.3_spmd.clone, body=%wide.region_0.2_spmd.clone.sunk | while | flops 203424880 | bytes 11670275 | solution.py:65
  24.7 3.5 scatter_fusion
  35.2 3.4 scatter_fusion
  45.6 3.3 scatter_fusion
  55.9 3.4 scatter_fusion
  97.1 3.4 scatter_fusion
  107.5 3.3 scatter_fusion
  117.8 3.3 scatter_fusion
  138.3 3.4 scatter_fusion
  158.9 3.4 scatter_fusion
  179.6 3.4 scatter_fusion
  189.9 3.4 scatter_fusion
  200.3 3.4 scatter_fusion
  210.6 3.4 scatter_fusion
  220.9 3.4 scatter_fusion
  231.2 3.4 scatter_fusion
  241.6 3.3 scatter_fusion
  251.9 3.4 scatter_fusion
  262.3 3.3 scatter_fusion
  272.6 3.4 scatter_fusion
  293.2 3.4 scatter_fusion
  297.8 66.9 %all-reduce.3.cloned.1.call-done = f32[3456,128]{1,0:T(8,128)} async-done(((f32[3456,128]{1,0:T(8,128)}), f32[3456,128]{1,0:T(8,128)}) %all-reduce.3.cloned.1.call-update) | async-done | bytes 1769488 | tf_op jit(solution)/shard_map/psum | solution.py:76
  373.1 58.1 %all-reduce.5.cloned.1.call-done = f32[3456,128]{1,0:T(8,128)} async-done(((f32[3456,128]{1,0:T(8,128)}), f32[3456,128]{1,0:T(8,128)}) %all-reduce.5.cloned.1.call-update) | async-done | bytes 1769488 | tf_op jit(solution)/shard_map/psum | solution.py:76
  (256 shorter events, 227.3 us)
Async XLA Ops:
  7.2 5.8 %copy-start.1 = (s32[1,16,27]{2,1,0:T(8,128)S(1)}, s32[1,16,27]{2,1,0:T(8,128)}, u32[]{:S(2)}) copy-start(s32[1,16,27]{2,1,0:T(8,128)} %param.14) | copy-start | bytes 5188
  7.2 357.6 %all-reduce.3.cloned.1.call-start = ((), (), s32[]{:S(2)}) async-start(), calls=%async_computation | async-start | bytes 3538944 | tf_op jit(solution)/shard_map/psum | solution.py:76
  9.2 3.8 collective-permute-start
  11.7 5.4 %collective-permute-start.1 = (bf16[4,128,128]{2,1,0:T(8,128)(2,1)S(1)}, bf16[4,128,128]{2,1,0:T(8,128)(2,1)S(1)}, u32[]{:S(2)}, u32[]{:S(2)}) collective-permute-start(bf16[4,128,128]{2,1,0:T(8,128)(2,1)S(1)} %get-tuple-element.241), channel_id=1, source_target_pairs={{1,0},{2,1},{3,2},{4,3},{5,4},{6,5},{7,6},{9,8},{10,9},{11,10},{12... | collective-permute-start | bytes 393224 | tf_op jit(solution)/shard_map/ppermute | solution.py:18
  297.7 67.0 %copy-start = (f32[24,128,128]{2,1,0:T(8,128)S(1)}, f32[24,128,128]{2,1,0:T(8,128)}, u32[]{:S(2)}) copy-start(f32[24,128,128]{2,1,0:T(8,128)} %get-tuple-element.184) | copy-start | bytes 4718596
  297.8 133.4 %all-reduce.5.cloned.1.call-start = ((), (), s32[]{:S(2)}) async-start(), calls=%async_computation.1 | async-start | bytes 3538944 | tf_op jit(solution)/shard_map/psum | solution.py:76
  364.9 2.7 collective-permute-start.2
  366.3 4.2 collective-permute-start.3
Sparse Core Ops, SparseCore 0:
  297.9 66.7 all-reduce.2
  367.9 63.2 all-reduce.4
